TPU v7x, 512 devices: a whole 4x8x8 slice. The times are simulated.
512 devices in a mesh: ep: 64 (over y, x, core), tp: 8 (over z).
Axes of the slice: x: 4, y: 8, z: 8, core: 2. Of those that a mesh axis runs over, the one named last changes fastest.
Arguments:
- attn: bfloat16 [512, 4096], P('ep', 'tp'), may hold values from -6 to 6
- resid: bfloat16 [512, 4096], P('ep'), may hold values from -3 to 3
- wo: bfloat16 [4096, 4096], P('tp', 'ep'), may hold values from -0.09375 to 0.09375
- norm_gain: float32 [4096], replicated, may hold values from 0.25 to 1.75
- router: bfloat16 [4096, 8], replicated, may hold values from -0.09375 to 0.09375
- expert_ids: int32 [512, 2], P('ep'), may hold values from 0 to 7, all different within a row; in each aligned block of 8 rows (0 to 7, 8 to 15, ...) at most 4 rows name the same one
- w_gate: bfloat16 [4096, 65536], P(None, ('ep', 'tp')), may hold values from -0.09375 to 0.09375
- w_up: bfloat16 [4096, 65536], P(None, ('ep', 'tp')), may hold values from -0.09375 to 0.09375
- w_down: bfloat16 [65536, 4096], P(('ep', 'tp')), may hold values from -0.1875 to 0.1875
- lengths: int32 [64, 4], P('ep'), may hold values from 1 to 4, 8 in all within a row
- final_gain: float32 [4096], replicated, may hold values from 0.25 to 1.75
- head: bfloat16 [16384, 4096], P(('ep', 'tp')), may hold values from -0.375 to 0.375
Outputs:
- mixed: bfloat16 [512, 4096], P('ep')
- max_logit: float32 [256], replicated
Inputs may be any that keep to these rules, and one draw needn't show every extreme that they name: `expert_ids`: the two ids of a row differ; among the 8 rows of one index of ep no expert is named by more than 4 rows, a bound that some block reaches. Each row of lengths sums to 8, and its largest entry is 4.
All inputs are finite; a program needn't handle non-finite values.
Results may differ from a plain program's by a relative error of at most 0.0075.
Values may be sent and summed in bfloat16 or wider, within the bound.
A program may use at most 192 MiB of HBM per device.

v0:
```python
import jax
import jax.numpy as jnp
from jax import lax
from jax.sharding import PartitionSpec as P


def rms_scale(values, gain):
    return values * lax.rsqrt(jnp.mean(values * values, axis=1, keepdims=True) + 1e-05) * gain


def local(
    attn, resid, wo, norm_gain, router, expert_ids, w_gate, w_up, w_down, lengths, final_gain, head
):
    row_count = resid.shape[0]
    width = resid.shape[1]
    ep_count = lax.axis_size("ep")
    expert_count = router.shape[1]
    group_size = ep_count // expert_count
    capacity = row_count // 2
    partial_proj = jnp.dot(
        attn, lax.all_gather(wo, "ep", axis=1, tiled=True), preferred_element_type=jnp.float32
    )
    proj = lax.psum(partial_proj, "tp")
    stream = resid.astype(jnp.float32) + proj
    normed = rms_scale(stream, norm_gain).astype(jnp.bfloat16)
    logits = jnp.dot(normed, router, preferred_element_type=jnp.float32)
    expert_range = jnp.arange(expert_count, dtype=jnp.int32)
    one_hot = (expert_ids[:, :, None] == expert_range).astype(jnp.float32)
    picked = jnp.sum(one_hot * logits[:, None, :], axis=2)
    first = 1.0 / (1.0 + jnp.exp(picked[:, 1] - picked[:, 0]))
    second = 1.0 / (1.0 + jnp.exp(picked[:, 0] - picked[:, 1]))
    both_weights = jnp.stack([first, second], axis=1)
    flat_hot = (expert_ids.reshape(-1)[:, None] == expert_range).astype(jnp.int32)
    earlier = jnp.cumsum(flat_hot, axis=0) - flat_hot
    slot_index = jnp.sum(earlier * flat_hot, axis=1)
    target = (expert_ids.reshape(-1) * capacity + slot_index).reshape(row_count, 2)
    slot_range = jnp.arange(expert_count * capacity, dtype=jnp.int32)
    placed = (target[:, :, None] == slot_range).astype(jnp.float32)
    dispatch_matrix = jnp.sum(placed, axis=1).astype(jnp.bfloat16)
    combine_matrix = jnp.sum(placed * both_weights[:, :, None], axis=1)
    send_rows = lax.dot_general(
        dispatch_matrix, normed, (((0,), (0,)), ((), ())), preferred_element_type=jnp.float32
    ).astype(jnp.bfloat16)
    per_expert = send_rows.reshape(expert_count, 1, capacity, width)
    outgoing = jnp.broadcast_to(per_expert, (expert_count, group_size, capacity, width))
    outgoing = outgoing.reshape(ep_count, capacity, width)
    arrived = lax.all_to_all(outgoing, "ep", split_axis=0, concat_axis=0, tiled=True)
    flat_rows = arrived.reshape(-1, width)
    gate = jnp.dot(flat_rows, w_gate, preferred_element_type=jnp.float32)
    upper = jnp.dot(flat_rows, w_up, preferred_element_type=jnp.float32)
    hidden = (jax.nn.silu(gate) * upper).astype(jnp.bfloat16)
    term = jnp.dot(hidden, w_down, preferred_element_type=jnp.float32).astype(jnp.bfloat16)
    term = term.reshape(arrived.shape[0], arrived.shape[1], width)
    returned = lax.all_to_all(term, "ep", split_axis=0, concat_axis=0, tiled=True)
    back_width = returned.shape[2]
    grouped = returned.reshape(expert_count, group_size, capacity, back_width).astype(jnp.float32)
    grouped = jnp.sum(grouped, axis=1).reshape(expert_count * capacity, back_width)
    expert_part = jnp.dot(
        combine_matrix, grouped, precision=lax.Precision.HIGHEST, preferred_element_type=jnp.float32
    )
    expert_total = lax.psum(expert_part, "tp")
    mixed = (stream + expert_total).astype(jnp.bfloat16)
    ends = jnp.cumsum(lengths[0]) - 1
    row_range = jnp.arange(row_count, dtype=jnp.int32)
    selector = (ends[:, None] == row_range).astype(jnp.bfloat16)
    last = jnp.dot(selector, mixed, preferred_element_type=jnp.float32)
    final = rms_scale(last, final_gain).astype(jnp.bfloat16)
    vocab_logits = lax.dot_general(
        lax.all_gather(final, "ep", axis=0, tiled=True),
        head,
        (((1,), (1,)), ((), ())),
        preferred_element_type=jnp.float32,
    )
    local_max = jnp.max(vocab_logits, axis=1)
    max_logit = lax.pmax(local_max, ("ep", "tp"))
    return (mixed, max_logit)


def solution(mesh):
    placed = (
        P("ep", "tp"),
        P("ep", None),
        P("tp", "ep"),
        P(),
        P(),
        P("ep", None),
        P(None, ("ep", "tp")),
        P(None, ("ep", "tp")),
        P(("ep", "tp"), None),
        P("ep", None),
        P(),
        P(("ep", "tp"), None),
    )
    return jax.shard_map(
        local, mesh=mesh, in_specs=placed, out_specs=(P("ep", None), P()), check_vma=False
    )
```

profile of v0, /device:TPU:1, one launch (start us, length us, event | category | flops | bytes accessed | tf_op | source)
XLA Modules:
  0.0 583.7 jit_solution(15072324507917972072)
XLA Ops:
  7.2 0.7 all-gather.4.cloned.1.call-update
  8.0 0.8 copy.24
  8.9 0.2 select_reduce_fusion.2
  9.2 92.4 %all-gather.4.cloned.1.call-done = bf16[512,4096]{0,1:T(8,128)(2,1)} async-done(((bf16[512,64]{0,1:T(8,128)(2,1)}), bf16[512,4096]{0,1:T(8,128)(2,1)}) %all-gather.4.cloned.1.call-update) | async-done | bytes 4194320 | tf_op jit(solution)/shard_map/all_gather | solution.py:21
  101.6 4.0 fusion.13
  105.7 71.1 %all-reduce.3.cloned.1.call-done = f32[8,4096]{1,0:T(8,128)} async-done(((f32[8,4096]{1,0:T(8,128)}), f32[8,4096]{1,0:T(8,128)}) %all-reduce.3.cloned.1.call-update) | async-done | bytes 131088 | tf_op jit(solution)/shard_map/psum | solution.py:23
  176.8 1.1 multiply_reduce_fusion
  177.9 1.0 multiply_convert_fusion
  178.9 0.1 fusion.14
  179.0 0.2 select_reduce_fusion.1
  179.3 0.3 convolution_convert_fusion.1
  179.6 0.1 broadcast_in_dim.4
  179.7 1.0 broadcast_in_dim.5
  180.7 64.7 %all_to_all.10 = bf16[64,4,4096]{2,1,0:T(4,128)(2,1)} all-to-all(bf16[64,4,4096]{2,1,0:T(4,128)(2,1)S(1)} %bitcast.25), channel_id=1, replica_groups=mesh['ep'=64,'tp'=8] {'ep'}, dimensions={0} | all-to-all | bytes 4194304 | tf_op jit(solution)/shard_map/all_to_all | solution.py:47
  245.4 2.5 reshape.76
  248.0 1.9 fusion.15
  249.9 3.9 convolution_convert_fusion
  253.8 4.1 reshape.77
  257.9 7.1 %all-to-all-start.1 = ((bf16[64,4,4096]{2,1,0:T(4,128)(2,1)}), bf16[64,4,4096]{2,1,0:T(4,128)(2,1)S(1)}, u32[]{:S(2)}, u32[]{:S(2)}) async-start(bf16[64,4,4096]{2,1,0:T(4,128)(2,1)} %reshape.77), calls=%async_computation.1 | async-start | bytes 4194304 | tf_op jit(solution)/shard_map/all_to_all | solution.py:54
  265.1 0.2 reduce-window.8
  265.3 49.5 %all-to-all-done.1 = bf16[64,4,4096]{2,1,0:T(4,128)(2,1)S(1)} async-done(((bf16[64,4,4096]{2,1,0:T(4,128)(2,1)}), bf16[64,4,4096]{2,1,0:T(4,128)(2,1)S(1)}, u32[]{:S(2)}, u32[]{:S(2)}) %all-to-all-start.1) | async-done | bytes 2097184 | tf_op jit(solution)/shard_map/all_to_all | solution.py:54
  314.7 1.9 convert_reduce_fusion
  316.6 1.2 reshape.78
  317.8 1.0 fusion.16
  318.9 68.8 %all-reduce.5.cloned.1.call-done = f32[8,4096]{1,0:T(8,128)} async-done(((f32[8,4096]{1,0:T(8,128)}), f32[8,4096]{1,0:T(8,128)}) %all-reduce.5.cloned.1.call-update) | async-done | bytes 131088 | tf_op jit(solution)/shard_map/psum | solution.py:61
  387.7 0.9 add_convert_fusion
  388.7 0.3 multiply_reduce_fusion.1
  389.0 0.7 fusion.7
  389.7 87.1 %all-gather.6.cloned.1.call-done = bf16[64,4,4096]{2,1,0:T(4,128)(2,1)} async-done(((bf16[1,4,4096]{2,1,0:T(4,128)(2,1)}), bf16[64,4,4096]{2,1,0:T(4,128)(2,1)}) %all-gather.6.cloned.1.call-update) | async-done | bytes 2097168 | tf_op jit(solution)/shard_map/all_gather | solution.py:69
  476.8 2.5 reshape.82
  479.4 0.8 convolution_reduce_fusion
  480.1 97.0 %pmax.7 = f32[256]{0:T(256)} all-reduce(f32[256]{0:T(256)S(1)} %convolution_reduce_fusion), channel_id=1, replica_groups=mesh['ep'=64,'tp'=8] {'ep','tp'}, use_global_device_ids=true, to_apply=%region_12.13 | all-reduce | flops 256 | bytes 2048 | tf_op jit(solution)/shard_map/pmax | solution.py:75
  (39 shorter events, 0.7 us)
Async XLA Ops:
  7.2 242.7 %copy-start = (bf16[128,4096]{1,0:T(8,128)(2,1)S(1)}, bf16[128,4096]{1,0:T(8,128)(2,1)}, u32[]{:S(2)}) copy-start(bf16[128,4096]{1,0:T(8,128)(2,1)} %param.20) | copy-start | bytes 3145732
  7.2 94.4 %all-gather.4.cloned.1.call-start = ((), (), s32[]{:S(2)}) async-start(), calls=%async_computation.2 | async-start | bytes 4259840 | tf_op jit(solution)/shard_map/all_gather | solution.py:21
  7.9 168.9 %all-reduce.3.cloned.1.call-start = ((), (), s32[]{:S(2)}) async-start(), calls=%async_computation.3 | async-start | bytes 262144 | tf_op jit(solution)/shard_map/psum | solution.py:23
  9.2 167.6 %copy-start.2 = (bf16[8,4096]{1,0:T(8,128)(2,1)S(1)}, bf16[8,4096]{1,0:T(8,128)(2,1)}, u32[]{:S(2)}) copy-start(bf16[8,4096]{1,0:T(8,128)(2,1)} %param.13) | copy-start | bytes 196612
  9.2 168.7 %copy-start.6 = (f32[4096]{0:T(1024)S(1)}, f32[4096]{0:T(1024)}, u32[]{:S(2)}) copy-start(f32[4096]{0:T(1024)} %param.15) | copy-start | bytes 49156
  9.2 169.7 %copy-start.5 = (bf16[4096,8]{0,1:T(8,128)(2,1)S(1)}, bf16[4096,8]{0,1:T(8,128)(2,1)}, u32[]{:S(2)}) copy-start(bf16[4096,8]{0,1:T(8,128)(2,1)} %param.16) | copy-start | bytes 196612
  9.2 169.8 %copy-start.8 = (s32[8,2]{0,1:T(2,128)S(1)}, s32[8,2]{0,1:T(2,128)}, u32[]{:S(2)}) copy-start(s32[8,2]{0,1:T(2,128)} %param.17) | copy-start | bytes 196
  257.9 7.2 %copy-start.9 = (s32[1,4]{1,0:T(1,128)S(1)}, s32[1,4]{1,0:T(1,128)}, u32[]{:S(2)}) copy-start(s32[1,4]{1,0:T(1,128)} %param.21) | copy-start | bytes 52
  257.9 56.8 %all-to-all-start.1 = ((bf16[64,4,4096]{2,1,0:T(4,128)(2,1)}), bf16[64,4,4096]{2,1,0:T(4,128)(2,1)S(1)}, u32[]{:S(2)}, u32[]{:S(2)}) async-start(bf16[64,4,4096]{2,1,0:T(4,128)(2,1)} %reshape.77), calls=%async_computation.1 | async-start | bytes 4194304 | tf_op jit(solution)/shard_map/all_to_all | solution.py:54
  265.0 122.7 %all-reduce.5.cloned.1.call-start = ((), (), s32[]{:S(2)}) async-start(), calls=%async_computation.4 | async-start | bytes 262144 | tf_op jit(solution)/shard_map/psum | solution.py:61
  265.3 122.4 %copy-start.1 = (f32[8,4096]{1,0:T(8,128)S(1)}, f32[8,4096]{1,0:T(8,128)}, u32[]{:S(2)}) copy-start(f32[8,4096]{1,0:T(8,128)} %all-reduce.3.cloned.1.call-done) | copy-start | bytes 393220
  265.3 123.7 %copy-start.7 = (f32[4096]{0:T(1024)S(1)}, f32[4096]{0:T(1024)}, u32[]{:S(2)}) copy-start(f32[4096]{0:T(1024)} %param.22) | copy-start | bytes 49156
  318.9 157.9 %all-gather.6.cloned.1.call-start = ((), (), s32[]{:S(2)}) async-start(), calls=%async_computation.5 | async-start | bytes 2129920 | tf_op jit(solution)/shard_map/all_gather | solution.py:69
  388.6 90.7 %copy-start.4 = (bf16[8,4096]{1,0:T(8,128)(2,1)}, bf16[8,4096]{1,0:T(8,128)(2,1)S(1)}, u32[]{:S(2)}) copy-start(bf16[8,4096]{1,0:T(8,128)(2,1)S(1)} %add_convert_fusion) | copy-start | bytes 196612
  389.7 89.6 %copy-start.3 = (bf16[32,4096]{1,0:T(8,128)(2,1)S(1)}, bf16[32,4096]{1,0:T(8,128)(2,1)}, u32[]{:S(2)}) copy-start(bf16[32,4096]{1,0:T(8,128)(2,1)} %param.23) | copy-start | bytes 786436
Sparse Core Ops, SparseCore 0:
  11.3 90.1 all-gather.3
  105.7 71.0 all-reduce.2
  319.0 68.6 all-reduce.4
  390.9 85.8 all-gather.5
where the time goes:
time: 584 us
  waiting for transfers between devices  369 us (63%)
  blocking collectives  162 us (28%)
  between operations  14 us (2%)
  local copies, waits for them, and re-layouts  12.6 us (2%)
  matrix products  12.4 us (2%)
  starting transfers between devices  7.25 us (1%)
  other arithmetic  6.28 us (1%)
    pmax x1, blocking collectives, local(): max_logit = lax.pmax(local_max, ('ep', 'tp'))  97 us
    all_gather x1, waiting for transfers between devices, local(): lax.all_gather(wo, 'ep', axis=1, tiled=True)  92.4 us
    all_gather x1, waiting for transfers between devices, local(): lax.all_gather(final, 'ep', axis=0, tiled=True)  87.1 us
    psum x1, waiting for transfers between devices, local(): proj = lax.psum(partial_proj, 'tp')  71.1 us
    psum x1, waiting for transfers between devices, local(): expert_total = lax.psum(expert_part, 'tp')  68.8 us
    all_to_all x1, blocking collectives, local(): lax.all_to_all(outgoing, 'ep', split_axis=0, concat_axis=0, tiled=True)  64.7 us
    all_to_all x1, waiting for transfers between devices, local(): lax.all_to_all(term, 'ep', split_axis=0, concat_axis=0, tiled=True)  49.5 us
  transfers between devices with their start and end apart: 5, of which 5 were waited for; matrix products, arithmetic and copies ran while one was open for 0% of the time, Pallas kernels for 0%

commit v1 on v0

--- a/solution.py
+++ b/solution.py
@@ -58,7 +58,7 @@
     expert_part = jnp.dot(
         combine_matrix, grouped, precision=lax.Precision.HIGHEST, preferred_element_type=jnp.float32
     )
-    expert_total = lax.psum(expert_part, "tp")
+    expert_total = jnp.sum(lax.all_gather(expert_part, axis_name="tp"), 0)
     mixed = (stream + expert_total).astype(jnp.bfloat16)
     ends = jnp.cumsum(lengths[0]) - 1
     row_range = jnp.arange(row_count, dtype=jnp.int32)

time: 584 us -> 544 us (0.932)
  waiting for transfers between devices: 369 us -> 283 us
  blocking collectives: 162 us -> 218 us
  starting transfers between devices: 7.25 us -> 0.16 us
    psum x1 -> x0, waiting for transfers between devices: 68.8 us -> none  [local(): expert_total = lax.psum(expert_part, 'tp')]
    all_to_all x0 -> x1, blocking collectives: none -> 56.5 us  [local(): lax.all_to_all(term, 'ep', split_axis=0, concat_axis=0, tiled=True)]
    all_to_all x1 -> x0, waiting for transfers between devices: 49.5 us -> none  [local(): lax.all_to_all(term, 'ep', split_axis=0, concat_axis=0, tiled=True)]
    all_gather x0 -> x1, waiting for transfers between devices: none -> 31.9 us  [local(): expert_total = jnp.sum(lax.all_gather(expert_part, axis_name='tp'), 0)]
    all_to_all x1 -> x0, starting transfers between devices: 7.09 us -> none  [local(): lax.all_to_all(term, 'ep', split_axis=0, concat_axis=0, tiled=True)]
  transfers between devices with their start and end apart: 5 -> 4, of which waited for: 5 -> 4; matrix products, arithmetic and copies ran while one was open for 0% -> 0% of each run, Pallas kernels for 0% -> 0%
where the time goes in v1:
time: 544 us; the launch traced here: 543 us
  waiting for transfers between devices  283 us (52%)
  blocking collectives  218 us (40%)
  between operations  14 us (3%)
  matrix products  12.4 us (2%)
  local copies, waits for them, and re-layouts  10.2 us (2%)
  other arithmetic  5.9 us (1%)
    pmax x1, blocking collectives, local(): max_logit = lax.pmax(local_max, ('ep', 'tp'))  97 us
    all_gather x1, waiting for transfers between devices, local(): lax.all_gather(wo, 'ep', axis=1, tiled=True)  92.4 us
    all_gather x1, waiting for transfers between devices, local(): lax.all_gather(final, 'ep', axis=0, tiled=True)  86.5 us
    psum x1, waiting for transfers between devices, local(): proj = lax.psum(partial_proj, 'tp')  71 us
    all_to_all x1, blocking collectives, local(): lax.all_to_all(outgoing, 'ep', split_axis=0, concat_axis=0, tiled=True)  64.7 us
    all_to_all x1, blocking collectives, local(): lax.all_to_all(term, 'ep', split_axis=0, concat_axis=0, tiled=True)  56.5 us
    all_gather x1, waiting for transfers between devices, local(): expert_total = jnp.sum(lax.all_gather(expert_part, axis_name='tp'), 0)  31.9 us
  transfers between devices with their start and end apart: 4, of which 4 were waited for; matrix products, arithmetic and copies ran while one was open for 0% of the time, Pallas kernels for 0%

profile of v1, /device:TPU:1, one launch (start us, length us, event | category | flops | bytes accessed | tf_op | source)
XLA Modules:
  0.0 543.3 jit_solution(13214055922841127720)
XLA Ops:
  7.2 0.7 all-gather.6.cloned.1.call-update
  8.0 0.8 copy.24
  8.9 0.2 select_reduce_fusion.2
  9.2 92.4 %all-gather.6.cloned.1.call-done = bf16[512,4096]{0,1:T(8,128)(2,1)} async-done(((bf16[512,64]{0,1:T(8,128)(2,1)}), bf16[512,4096]{0,1:T(8,128)(2,1)}) %all-gather.6.cloned.1.call-update) | async-done | bytes 4194320 | tf_op jit(solution)/shard_map/all_gather | solution.py:21
  101.6 4.0 fusion.13
  105.7 0.1 copy.26
  105.8 71.0 %all-reduce.2.cloned.1.call-done = f32[8,4096]{1,0:T(8,128)} async-done(((f32[8,4096]{1,0:T(8,128)}), f32[8,4096]{1,0:T(8,128)}) %all-reduce.2.cloned.1.call-update) | async-done | bytes 131088 | tf_op jit(solution)/shard_map/psum | solution.py:23
  176.8 1.1 multiply_reduce_fusion
  177.9 1.0 multiply_convert_fusion
  178.9 0.1 fusion.14
  179.0 0.2 select_reduce_fusion.1
  179.3 0.3 convolution_convert_fusion.1
  179.6 0.1 broadcast_in_dim.4
  179.7 1.0 broadcast_in_dim.5
  180.7 64.7 %all_to_all.10 = bf16[64,4,4096]{2,1,0:T(4,128)(2,1)} all-to-all(bf16[64,4,4096]{2,1,0:T(4,128)(2,1)S(1)} %bitcast.27), channel_id=1, replica_groups=mesh['ep'=64,'tp'=8] {'ep'}, dimensions={0} | all-to-all | bytes 4194304 | tf_op jit(solution)/shard_map/all_to_all | solution.py:47
  245.4 2.5 reshape.76
  248.0 1.9 fusion.15
  249.9 3.9 convolution_convert_fusion
  253.8 2.7 reshape.77
  256.6 56.5 %all_to_all.11 = bf16[64,4,4096]{2,1,0:T(4,128)(2,1)S(1)} all-to-all(bf16[64,4,4096]{2,1,0:T(4,128)(2,1)S(1)} %reshape.77), channel_id=1, replica_groups=mesh['ep'=64,'tp'=8] {'ep'}, dimensions={0} | all-to-all | bytes 4194304 | tf_op jit(solution)/shard_map/all_to_all | solution.py:54
  313.0 1.1 convert_reduce_fusion
  314.2 0.2 reshape.78
  314.3 1.0 fusion.16
  315.4 0.2 reduce-window.8
  315.6 31.9 %all-gather.8.cloned.1.call-done = f32[64,4096]{1,0:T(8,128)} async-done(((f32[8,4096]{1,0:T(8,128)}), f32[64,4096]{1,0:T(8,128)}) %all-gather.8.cloned.1.call-update) | async-done | bytes 1048592 | tf_op jit(solution)/shard_map/all_gather | solution.py:61
  347.5 1.3 bitcast_reduce_fusion
  348.8 0.3 multiply_reduce_fusion.1
  349.2 0.7 fusion.7
  349.9 86.5 %all-gather.10.cloned.1.call-done = bf16[64,4,4096]{2,1,0:T(4,128)(2,1)} async-done(((bf16[1,4,4096]{2,1,0:T(4,128)(2,1)}), bf16[64,4,4096]{2,1,0:T(4,128)(2,1)}) %all-gather.10.cloned.1.call-update) | async-done | bytes 2097168 | tf_op jit(solution)/shard_map/all_gather | solution.py:69
  436.5 2.5 reshape.83
  439.0 0.8 convolution_reduce_fusion
  439.8 97.0 %pmax.7 = f32[256]{0:T(256)} all-reduce(f32[256]{0:T(256)S(1)} %convolution_reduce_fusion), channel_id=1, replica_groups=mesh['ep'=64,'tp'=8] {'ep','tp'}, use_global_device_ids=true, to_apply=%region_12.13 | all-reduce | flops 256 | bytes 2048 | tf_op jit(solution)/shard_map/pmax | solution.py:75
  (39 shorter events, 0.7 us)
Async XLA Ops:
  7.2 242.7 %copy-start = (bf16[128,4096]{1,0:T(8,128)(2,1)S(1)}, bf16[128,4096]{1,0:T(8,128)(2,1)}, u32[]{:S(2)}) copy-start(bf16[128,4096]{1,0:T(8,128)(2,1)} %param.20) | copy-start | bytes 3145732
  7.2 94.4 %all-gather.6.cloned.1.call-start = ((), (), s32[]{:S(2)}) async-start(), calls=%async_computation.2 | async-start | bytes 4259840 | tf_op jit(solution)/shard_map/all_gather | solution.py:21
  7.9 168.9 %all-reduce.2.cloned.1.call-start = ((), (), s32[]{:S(2)}) async-start(), calls=%async_computation.3 | async-start | bytes 262144 | tf_op jit(solution)/shard_map/psum | solution.py:23
  9.2 167.6 %copy-start.2 = (bf16[8,4096]{1,0:T(8,128)(2,1)S(1)}, bf16[8,4096]{1,0:T(8,128)(2,1)}, u32[]{:S(2)}) copy-start(bf16[8,4096]{1,0:T(8,128)(2,1)} %param.13) | copy-start | bytes 196612
  9.2 168.7 %copy-start.6 = (f32[4096]{0:T(1024)S(1)}, f32[4096]{0:T(1024)}, u32[]{:S(2)}) copy-start(f32[4096]{0:T(1024)} %param.15) | copy-start | bytes 49156
  9.2 169.7 %copy-start.5 = (bf16[4096,8]{0,1:T(8,128)(2,1)S(1)}, bf16[4096,8]{0,1:T(8,128)(2,1)}, u32[]{:S(2)}) copy-start(bf16[4096,8]{0,1:T(8,128)(2,1)} %param.16) | copy-start | bytes 196612
  9.2 169.8 %copy-start.8 = (s32[8,2]{0,1:T(2,128)S(1)}, s32[8,2]{0,1:T(2,128)}, u32[]{:S(2)}) copy-start(s32[8,2]{0,1:T(2,128)} %param.17) | copy-start | bytes 196
  105.6 241.9 %all-gather.8.cloned.1.call-start = ((), (), s32[]{:S(2)}) async-start(), calls=%async_computation.4 | async-start | bytes 1179648 | tf_op jit(solution)/shard_map/all_gather | solution.py:61
  313.0 2.4 copy-start.9
  314.1 34.6 %copy-start.1 = (f32[8,4096]{1,0:T(8,128)S(1)}, f32[8,4096]{1,0:T(8,128)}, u32[]{:S(2)}) copy-start(f32[8,4096]{1,0:T(8,128)} %all-reduce.2.cloned.1.call-done) | copy-start | bytes 393220
  314.1 35.0 %copy-start.7 = (f32[4096]{0:T(1024)S(1)}, f32[4096]{0:T(1024)}, u32[]{:S(2)}) copy-start(f32[4096]{0:T(1024)} %param.22) | copy-start | bytes 49156
  315.4 121.1 %all-gather.10.cloned.1.call-start = ((), (), s32[]{:S(2)}) async-start(), calls=%async_computation.5 | async-start | bytes 2129920 | tf_op jit(solution)/shard_map/all_gather | solution.py:69
  348.8 90.2 %copy-start.4 = (bf16[8,4096]{1,0:T(8,128)(2,1)}, bf16[8,4096]{1,0:T(8,128)(2,1)S(1)}, u32[]{:S(2)}) copy-start(bf16[8,4096]{1,0:T(8,128)(2,1)S(1)} %add_convert_fusion) | copy-start | bytes 196612
  349.9 89.1 %copy-start.3 = (bf16[32,4096]{1,0:T(8,128)(2,1)S(1)}, bf16[32,4096]{1,0:T(8,128)(2,1)}, u32[]{:S(2)}) copy-start(bf16[32,4096]{1,0:T(8,128)(2,1)} %param.23) | copy-start | bytes 786436
Sparse Core Ops, SparseCore 0:
  11.3 90.1 all-gather.5
  105.7 71.0 all-reduce.1
  315.5 31.9 all-gather.7
  350.7 85.7 all-gather.9
